TPU v7x, 32 devices: a whole 2x2x4 slice. The times are simulated.
32 devices in a mesh: groups: 2 (over x), row: 16 (over z, y, core).
Axes of the slice: x: 2, y: 2, z: 4, core: 2. Of those that a mesh axis runs over, the one named last changes fastest.
Arguments:
- design_matrix: bfloat16 [1024, 65536], P('groups', 'row'), parts along dimension 0, may hold values from -0.0546875 to 0.0546875
- targets: float32 [1024, 128], P(('groups', 'row')), parts along dimension 0, may hold values from -24 to 24
- linear: float32 [131072, 128], P(('groups', 'row')), parts along dimension 0, may hold values from -24 to 24
- diagonal: float32 [131072], P(('groups', 'row')), parts along dimension 0, may hold values from 0.1 to 2
- lower_code: int32 [131072, 128], P(('groups', 'row')), parts along dimension 0, may hold values from -192 to -17
- upper_code: int32 [131072, 128], P(('groups', 'row')), parts along dimension 0, may hold values from 16 to 191
Outputs:
- box_iterate: float32 [131072, 128], P(('groups', 'row')), parts along dimension 0
- scaled_dual: float32 [131072, 128], P(('groups', 'row')), parts along dimension 0
There are 2 independent parts, one for each index of `groups`. A program takes and returns all parts, laid end to end along the dimension named above; each array names one. Nothing has to cross between parts.
All inputs are finite; a program needn't handle non-finite values.
Results may differ from a plain program's by a relative error of at most 0.00033.
Values may be sent and summed in bfloat16 or wider, within the bound.
No kernel may reach another device: no remote copies, remote signals or barrier semaphores. Data moves between devices by JAX's collectives and lax.ppermute only.
A program may use at most 128 MiB of HBM per device.

v0:
```python
import jax
import jax.numpy as jnp
from jax import lax
from jax.sharding import PartitionSpec as P

ITERS = 4


rho_plus_lip = 7.0


def solve_small(matrix, rhs):
    count = len(rhs)
    table = [list(line) for line in matrix]
    right = list(rhs)
    for p in range(count):
        for i in range(p + 1, count):
            factor = table[i][p] / table[p][p]
            for j in range(p, count):
                table[i][j] = table[i][j] - factor * table[p][j]
            right[i] = right[i] - factor * right[p]
    result = [None] * count
    for i in reversed(range(count)):
        total = right[i]
        for j in range(i + 1, count):
            total = total - table[i][j] * result[j]
        result[i] = total / table[i][i]
    return result


def mix_weights(gram):
    count = len(gram)
    trace = gram[0][0]
    for i in range(1, count):
        trace = trace + gram[i][i]
    shift = 0.01 * trace / count + 1e-06
    matrix = [[gram[i][j] + (shift if i == j else 0.0) for j in range(count)] for i in range(count)]
    solved = solve_small(matrix, [jnp.ones_like(trace)] * count)
    total = solved[0]
    for i in range(1, count):
        total = total + solved[i]
    return [item / total for item in solved]


def per_device(design_matrix, targets, linear, diagonal, lower_code, upper_code):
    lower = lower_code.astype(jnp.float32) / 64.0
    upper = upper_code.astype(jnp.float32) / 64.0
    step_size = (1.0 / (rho_plus_lip + diagonal))[:, None]
    state = jnp.zeros((2,) + linear.shape, jnp.float32)
    hist_mapped = []
    hist_change = []
    gram = []
    for iteration in range(ITERS):
        point = state[0] - state[1]
        point_b = point.astype(jnp.bfloat16)
        product = lax.psum_scatter(
            jnp.dot(design_matrix, point_b, preferred_element_type=jnp.float32),
            "row",
            scatter_dimension=0,
            tiled=True,
        )
        misfit = (product - targets).astype(jnp.bfloat16)
        gradient = lax.dot_general(
            design_matrix,
            lax.all_gather(misfit, "row", axis=0, tiled=True),
            (((0,), (0,)), ((), ())),
            preferred_element_type=jnp.float32,
        )
        gradient = gradient + diagonal[:, None] * point + linear
        moved = point - step_size * gradient
        boxed = jnp.clip(moved + state[1], lower, upper)
        scaled = state[1] + moved - boxed
        mapped = jnp.stack([boxed, scaled])
        change = mapped - state
        hist_mapped.append(mapped)
        hist_change.append(change)
        count = len(hist_change)
        stacked = jnp.stack(hist_change)
        partial_all = jnp.einsum(
            "icns,jcns->ijs", stacked, stacked, precision=lax.Precision.HIGHEST
        )
        whole = lax.psum(partial_all, "row")
        gram = [[whole[i, j] for j in range(count)] for i in range(count)]
        alpha = mix_weights(gram)
        combined = alpha[0][None, None, :] * hist_mapped[0]
        for i in range(1, count):
            combined = combined + alpha[i][None, None, :] * hist_mapped[i]
        state = jnp.stack([jnp.clip(combined[0], lower, upper), combined[1]])
    return (state[0], state[1])


def solution(mesh):
    in_specs = (
        P("groups", "row"),
        P(("groups", "row"), None),
        P(("groups", "row"), None),
        P(("groups", "row")),
        P(("groups", "row"), None),
        P(("groups", "row"), None),
    )
    out_specs = (P(("groups", "row"), None), P(("groups", "row"), None))
    return jax.shard_map(
        per_device, mesh=mesh, in_specs=in_specs, out_specs=out_specs, check_vma=False
    )
```

profile of v0, /device:TPU:0, one launch (start us, length us, event | category | flops | bytes accessed | tf_op | source)
XLA Modules:
  0.0 811.2 jit_solution(4368304568969252268)
XLA Ops:
  7.2 3.7 convolution_bitcast_fusion.6
  11.9 1.9 copy.60
  13.8 2.9 copy.59
  16.7 2.9 copy.63
  19.6 50.7 %reduce-scatter.13.cloned.1.call-done = f32[32,128]{1,0:T(8,128)} async-done(((f32[512,128]{1,0:T(8,128)}), f32[32,128]{1,0:T(8,128)}) %reduce-scatter.13.cloned.1.call-update) | async-done | bytes 16400
  71.3 19.8 %all_gather.12 = bf16[512,128]{1,0:T(8,128)(2,1)S(1)} all-gather(bf16[32,128]{1,0:T(8,128)(2,1)S(1)} %copy.62), channel_id=1, replica_groups=mesh['groups'=2,'row'=16] {'row'}, dimensions={0}, use_global_device_ids=true | all-gather | bytes 139264 | tf_op jit(solution)/shard_map/all_gather | solution.py:65
  91.0 4.8 fusion.49
  96.3 1.0 copy-done.10
  97.9 29.8 %psum.28 = f32[1,1,128]{2,1,0:T(1,128)S(1)} all-reduce(f32[1,1,128]{2,1,0:T(1,128)S(1)} %bitcast.204), channel_id=1, replica_groups=mesh['groups'=2,'row'=16] {'row'}, use_global_device_ids=true, to_apply=%region_1.2 | all-reduce | flops 128 | bytes 1024 | tf_op jit(solution)/shard_map/psum | solution.py:82
  127.7 5.2 fusion.51
  133.4 1.7 copy-done.21
  135.0 1.4 copy-done.26
  136.4 0.9 copy-done
  137.4 1.6 convolution_bitcast_fusion.5
  138.9 0.9 copy.94
  139.9 3.2 slice_bitcast_fusion.7
  143.1 49.9 %reduce-scatter.15.cloned.1.call-done = f32[32,128]{1,0:T(8,128)} async-done(((f32[512,128]{1,0:T(8,128)}), f32[32,128]{1,0:T(8,128)}) %reduce-scatter.15.cloned.1.call-update) | async-done | bytes 16400
  193.9 19.8 %all_gather.13 = bf16[512,128]{1,0:T(8,128)(2,1)S(1)} all-gather(bf16[32,128]{1,0:T(8,128)(2,1)S(1)} %copy.65), channel_id=1, replica_groups=mesh['groups'=2,'row'=16] {'row'}, dimensions={0}, use_global_device_ids=true | all-gather | bytes 139264 | tf_op jit(solution)/shard_map/all_gather | solution.py:65
  213.7 5.4 fusion.22
  219.7 1.6 subtract_bitcast_fusion.5
  221.8 1.0 copy-done.27
  224.1 3.1 copy-done.16
  227.1 1.0 pad_maximum_fusion.2
  228.1 75.1 %fusion.43 = f32[128,2,2]{2,1,0:T(2,128)S(1)} fusion(f32[2,2,4096,128]{2,3,1,0:T(8,128)S(1)} %pad_maximum_fusion.2), kind=kOutput, calls=%fused_computation.79 | convolution fusion | flops 50331648 | bytes 8390656 | tf_op jit(solution)/shard_map/icns,jcns->ijs/dot_general | solution.py:79
  303.4 29.8 %psum.29 = f32[2,2,128]{2,1,0:T(2,128)S(1)} all-reduce(f32[2,2,128]{2,1,0:T(2,128)S(1)} %bitcast.203), channel_id=1, replica_groups=mesh['groups'=2,'row'=16] {'row'}, use_global_device_ids=true, to_apply=%region_3.4 | all-reduce | flops 512 | bytes 4096 | tf_op jit(solution)/shard_map/psum | solution.py:82
  333.2 4.5 multiply_add_fusion.1
  338.2 1.7 copy-done.20
  339.9 1.4 copy-done.28
  341.3 1.0 copy-done.1
  342.2 1.6 convolution_bitcast_fusion.4
  343.8 0.9 copy.96
  344.7 3.2 slice_bitcast_fusion.6
  347.9 49.9 %reduce-scatter.17.cloned.1.call-done = f32[32,128]{1,0:T(8,128)} async-done(((f32[512,128]{1,0:T(8,128)}), f32[32,128]{1,0:T(8,128)}) %reduce-scatter.17.cloned.1.call-update) | async-done | bytes 16400
  398.7 19.8 %all_gather.14 = bf16[512,128]{1,0:T(8,128)(2,1)S(1)} all-gather(bf16[32,128]{1,0:T(8,128)(2,1)S(1)} %copy.71), channel_id=1, replica_groups=mesh['groups'=2,'row'=16] {'row'}, dimensions={0}, use_global_device_ids=true | all-gather | bytes 139264 | tf_op jit(solution)/shard_map/all_gather | solution.py:65
  418.5 5.3 fusion.23
  424.5 1.5 subtract_bitcast_fusion.3
  426.6 1.0 copy-done.29
  428.3 2.6 maximum_subtract_fusion.1
  430.9 1.1 copy-done.14
  432.0 9.3 %pad_maximum_fusion.1 = f32[3,2,4096,128]{2,3,1,0:T(8,128)} fusion(f32[1,2,4096,128]{2,3,1,0:T(8,128)} %maximum_subtract_fusion.1, f32[1,2,4096,128]{2,3,1,0:T(8,128)S(1)} %copy-done.14, f32[1,2,4096,128]{2,3,1,0:T(8,128)} %get-tuple-element.57), kind=kLoop, calls=%fused_computation.5 | loop fusion | flops 6291456 | bytes 25165824 | tf_op jit(solution)/shard_map/stack | solution.py:78
  441.2 102.3 %fusion.37 = f32[128,3,3]{2,1,0:T(4,128)S(1)} fusion(f32[3,2,4096,128]{2,3,1,0:T(8,128)} %pad_maximum_fusion.1), kind=kOutput, calls=%fused_computation.77 | convolution fusion | flops 113246208 | bytes 12587520 | tf_op jit(solution)/shard_map/icns,jcns->ijs/dot_general | solution.py:79
  543.6 30.3 %psum.30 = f32[3,3,128]{2,1,0:T(4,128)S(1)} all-reduce(f32[3,3,128]{2,1,0:T(4,128)S(1)} %bitcast.202), channel_id=1, replica_groups=mesh['groups'=2,'row'=16] {'row'}, use_global_device_ids=true, to_apply=%region_5.6 | all-reduce | flops 1152 | bytes 9216 | tf_op jit(solution)/shard_map/psum | solution.py:82
  574.1 5.4 multiply_add_fusion
  580.1 1.6 copy-done.19
  581.7 1.4 copy-done.24
  583.1 0.9 copy-done.2
  584.0 1.5 convolution_bitcast_fusion.3
  586.4 3.2 slice_bitcast_fusion.5
  589.6 50.0 %reduce-scatter.19.cloned.1.call-done = f32[32,128]{1,0:T(8,128)} async-done(((f32[512,128]{1,0:T(8,128)}), f32[32,128]{1,0:T(8,128)}) %reduce-scatter.19.cloned.1.call-update) | async-done | bytes 16400
  640.4 19.8 %all_gather.15 = bf16[512,128]{1,0:T(8,128)(2,1)S(1)} all-gather(bf16[32,128]{1,0:T(8,128)(2,1)S(1)} %copy.77), channel_id=1, replica_groups=mesh['groups'=2,'row'=16] {'row'}, dimensions={0}, use_global_device_ids=true | all-gather | bytes 139264 | tf_op jit(solution)/shard_map/all_gather | solution.py:65
  660.2 5.4 fusion.24
  666.2 1.6 subtract_bitcast_fusion.1
  668.3 1.0 copy-done.25
  669.9 2.6 maximum_subtract_fusion.2
  672.5 1.1 copy-done.15
  673.6 1.3 copy-done.17
  674.9 1.2 copy-done.22
  676.1 4.0 pad_maximum_fusion
  680.1 80.1 %fusion.40 = f32[128,4,4]{2,1,0:T(4,128)S(1)} fusion(f32[4,2,4096,128]{2,3,1,0:T(8,128)S(1)} %pad_maximum_fusion), kind=kOutput, calls=%fused_computation.78 | convolution fusion | flops 201326592 | bytes 16785408 | tf_op jit(solution)/shard_map/icns,jcns->ijs/dot_general | solution.py:79
  760.2 30.3 %psum.31 = f32[4,4,128]{2,1,0:T(4,128)S(1)} all-reduce(f32[4,4,128]{2,1,0:T(4,128)S(1)} %bitcast.201), channel_id=1, replica_groups=mesh['groups'=2,'row'=16] {'row'}, use_global_device_ids=true, to_apply=%region_7.8 | all-reduce | flops 2048 | bytes 16384 | tf_op jit(solution)/shard_map/psum | solution.py:82
  790.7 6.9 fusion.25
  797.6 1.9 fusion.27
  799.7 1.8 copy.83
  801.5 2.9 copy.82
  (100 shorter events, 14.7 us)
Async XLA Ops:
  7.2 4.6 copy-start.34
  7.2 63.2 %reduce-scatter.13.cloned.1.call-start = ((), (), s32[]{:S(2)}) async-start(), calls=%async_computation.4 | async-start | bytes 278528
  11.8 181.2 %reduce-scatter.15.cloned.1.call-start = ((), (), s32[]{:S(2)}) async-start(), calls=%async_computation.5 | async-start | bytes 278528
  16.7 2.9 copy-start.33
  95.9 1.4 copy-start.10
  95.9 2.0 copy-start.11
  127.7 5.2 copy-start.3
  132.9 2.1 copy-start.21
  132.9 4.5 copy-start
  135.0 1.4 copy-start.26
  139.8 258.0 %reduce-scatter.17.cloned.1.call-start = ((), (), s32[]{:S(2)}) async-start(), calls=%async_computation.6 | async-start | bytes 278528
  213.7 5.4 copy-start.4
  219.7 2.1 copy-start.12
  219.7 3.1 copy-start.27
  219.7 3.7 copy-start.31
  223.4 3.7 copy-start.16
  224.1 4.1 copy-start.13
  333.2 4.5 copy-start.5
  337.7 2.1 copy-start.20
  337.8 4.5 copy-start.1
  339.9 1.4 copy-start.28
  344.7 294.9 %reduce-scatter.19.cloned.1.call-start = ((), (), s32[]{:S(2)}) async-start(), calls=%async_computation.7 | async-start | bytes 278528
  418.5 5.4 copy-start.6
  424.5 2.1 copy-start.18
  424.5 3.1 copy-start.29
  424.5 3.7 copy-start.32
  428.3 3.7 copy-start.14
  574.0 5.5 copy-start.7
  579.5 2.1 copy-start.19
  579.5 4.5 copy-start.2
  581.7 1.4 copy-start.24
  660.2 5.4 copy-start.8
  666.2 2.1 copy-start.23
  666.2 3.1 copy-start.25
  666.2 3.7 copy-start.30
  669.9 3.7 copy-start.15
  669.9 5.0 copy-start.17
  669.9 6.2 copy-start.22
  790.7 6.9 copy-start.9
Sparse Core Ops, SparseCore 0:
  11.9 58.4 reduce-scatter.12
  139.9 52.9 reduce-scatter.14
  344.8 52.9 reduce-scatter.16
  586.5 52.9 reduce-scatter.18
where the time goes:
time: 819 us; the launch traced here: 811 us
  matrix products  287 us (35%)
  waiting for transfers between devices  201 us (25%)
  blocking collectives  200 us (24%)
  local copies, waits for them, and re-layouts  57.2 us (7%)
  other arithmetic  52.6 us (6%)
  between operations  14.5 us (2%)
    dot_general x3, matrix products, per_device(): jnp.einsum('icns,jcns->ijs', stacked, stacked, precision=lax.Precision.HI...  257 us
    unnamed x8, waiting for transfers between devices  201 us
    psum x4, blocking collectives, per_device(): whole = lax.psum(partial_all, 'row')  120 us
    all_gather x4, blocking collectives, per_device(): lax.all_gather(misfit, 'row', axis=0, tiled=True)  79.2 us
    unnamed x84, local copies, waits for them, and re-layouts  46.9 us
    dot_general x4, matrix products, per_device(): lax.dot_general(design_matrix, lax.all_gather(misfit, 'row', axis=0, tile...  20.9 us
    another operation x4, other arithmetic, per_device(): stacked = jnp.stack(hist_change)  19.4 us
    add x3, other arithmetic, per_device(): combined = combined + alpha[i][None, None, :] * hist_mapped[i]  16.8 us
  transfers between devices with their start and end apart: 4, of which 4 were waited for; matrix products, arithmetic and copies ran while one was open for 2% of the time, Pallas kernels for 0%

commit v1 on v0

v1 whole, which is shorter than its diff:
```python
import jax
import jax.numpy as jnp
from jax import lax
from jax.sharding import PartitionSpec as P

ITERS = 4


rho_plus_lip = 7.0


def solve_small(matrix, rhs):
    count = len(rhs)
    table = [list(line) for line in matrix]
    right = list(rhs)
    for p in range(count):
        for i in range(p + 1, count):
            factor = table[i][p] / table[p][p]
            for j in range(p, count):
                table[i][j] = table[i][j] - factor * table[p][j]
            right[i] = right[i] - factor * right[p]
    result = [None] * count
    for i in reversed(range(count)):
        total = right[i]
        for j in range(i + 1, count):
            total = total - table[i][j] * result[j]
        result[i] = total / table[i][i]
    return result


def mix_weights(gram):
    count = len(gram)
    trace = gram[0][0]
    for i in range(1, count):
        trace = trace + gram[i][i]
    shift = 0.01 * trace / count + 1e-06
    matrix = [[gram[i][j] + (shift if i == j else 0.0) for j in range(count)] for i in range(count)]
    solved = solve_small(matrix, [jnp.ones_like(trace)] * count)
    total = solved[0]
    for i in range(1, count):
        total = total + solved[i]
    return [item / total for item in solved]


def apply_map(design_matrix, misfit, z, u, linear, diag, step_size, lower, upper):
    gradient = lax.dot_general(
        design_matrix,
        misfit,
        (((0,), (0,)), ((), ())),
        preferred_element_type=jnp.float32,
    )
    point = z - u
    gradient = gradient + diag * point + linear
    moved = point - step_size * gradient
    boxed = jnp.clip(moved + u, lower, upper)
    return boxed, u + moved - boxed


def per_device(design_matrix, targets, linear, diagonal, lower_code, upper_code):
    lower = lower_code.astype(jnp.float32) / 64.0
    upper = upper_code.astype(jnp.float32) / 64.0
    diag = diagonal[:, None]
    step_size = 1.0 / (rho_plus_lip + diag)
    z = jnp.zeros(linear.shape, jnp.float32)
    u = z
    mapped = []
    change = []
    gram = {}
    fresh = []
    for iteration in range(ITERS):
        if iteration == 0:
            misfit = (-targets).astype(jnp.bfloat16)
        else:
            product = lax.psum_scatter(
                jnp.dot(
                    design_matrix,
                    (z - u).astype(jnp.bfloat16),
                    preferred_element_type=jnp.float32,
                ),
                "row",
                scatter_dimension=0,
                tiled=True,
            )
            misfit = (product - targets).astype(jnp.bfloat16)
        misfit = lax.all_gather(misfit, "row", axis=0, tiled=True)
        boxed, scaled = apply_map(
            design_matrix, misfit, z, u, linear, diag, step_size, lower, upper
        )
        mapped.append((boxed, scaled))
        change.append((boxed - z, scaled - u))
        for i in range(iteration + 1):
            fresh.append(
                (
                    (i, iteration),
                    jnp.sum(
                        change[i][0] * change[iteration][0]
                        + change[i][1] * change[iteration][1],
                        axis=0,
                    ),
                )
            )
        if iteration == 0:
            z, u = boxed, scaled
            continue
        partial = jnp.stack([item for _, item in fresh])
        whole = jnp.sum(lax.all_gather(partial, "row", axis=0), axis=0)
        for k, (pair, _) in enumerate(fresh):
            gram[pair] = whole[k]
        fresh = []
        count = iteration + 1
        alpha = mix_weights(
            [
                [gram[(min(i, j), max(i, j))] for j in range(count)]
                for i in range(count)
            ]
        )
        z = alpha[0][None, :] * mapped[0][0]
        u = alpha[0][None, :] * mapped[0][1]
        for i in range(1, count):
            z = z + alpha[i][None, :] * mapped[i][0]
            u = u + alpha[i][None, :] * mapped[i][1]
        z = jnp.clip(z, lower, upper)
    return z, u


def solution(mesh):
    in_specs = (
        P("groups", "row"),
        P(("groups", "row"), None),
        P(("groups", "row"), None),
        P(("groups", "row")),
        P(("groups", "row"), None),
        P(("groups", "row"), None),
    )
    out_specs = (P(("groups", "row"), None), P(("groups", "row"), None))
    return jax.shard_map(
        per_device, mesh=mesh, in_specs=in_specs, out_specs=out_specs, check_vma=False
    )
```

time: 819 us -> 379 us (0.46)
  matrix products: 287 us -> 45.2 us
  blocking collectives: 200 us -> 135 us
  local copies, waits for them, and re-layouts: 57.2 us -> 3.48 us
  waiting for transfers between devices: 201 us -> 162 us
  other arithmetic: 52.6 us -> 19.1 us
    dot_general x11 -> x7, matrix products: 287 us -> 45.2 us  [the longest x4 34.4 us: apply_map(): lax.dot_general(design_matrix, misfit, (((0,), (0,)), ((), ())), preferre...]
    unnamed x8 -> x3, waiting for transfers between devices: 201 us -> 0.05 us
    reduce_scatter x0 -> x3, waiting for transfers between devices: none -> 162 us  [per_device(): lax.psum_scatter(jnp.dot(design_matrix, (z - u).astype(jnp.bfloat16), pre...]
    psum x4 -> x0, blocking collectives: 120 us -> none  [per_device(): whole = lax.psum(partial_all, 'row')]
    all_gather x4 -> x7, blocking collectives: 79.2 us -> 135 us  [the longest x4 82.7 us: per_device(): misfit = lax.all_gather(misfit, 'row', axis=0, tiled=True)]
    unnamed x84 -> x22, local copies, waits for them, and re-layouts: 46.9 us -> 3.48 us
    another operation x10 -> x0, other arithmetic: 26 us -> none  [the longest x4 19.4 us: per_device(): stacked = jnp.stack(hist_change)]
    add x3 -> x1, other arithmetic: 16.8 us -> 6.92 us  [per_device(): u = u + alpha[i][None, :] * mapped[i][1]]
  transfers between devices with their start and end apart: 4 -> 3, of which waited for: 4 -> 3; matrix products, arithmetic and copies ran while one was open for 2% -> 0% of each run, Pallas kernels for 0% -> 0%
where the time goes in v1:
time: 379 us
  waiting for transfers between devices  162 us (43%)
  blocking collectives  135 us (36%)
  matrix products  45.2 us (12%)
  other arithmetic  19.1 us (5%)
  between operations  13.9 us (4%)
    reduce_scatter x3, waiting for transfers between devices, per_device(): lax.psum_scatter(jnp.dot(design_matrix, (z - u).astype(jnp.bfloat16), pre...  162 us
    all_gather x4, blocking collectives, per_device(): misfit = lax.all_gather(misfit, 'row', axis=0, tiled=True)  82.7 us
    all_gather x3, blocking collectives, per_device(): whole = jnp.sum(lax.all_gather(partial, 'row', axis=0), axis=0)  52.7 us
    dot_general x4, matrix products, apply_map(): lax.dot_general(design_matrix, misfit, (((0,), (0,)), ((), ())), preferre...  34.4 us
    dot_general x3, matrix products, per_device(): jnp.dot(design_matrix, (z - u).astype(jnp.bfloat16), preferred_element_ty...  10.8 us
  transfers between devices with their start and end apart: 3, of which 3 were waited for; matrix products, arithmetic and copies ran while one was open for 0% of the time, Pallas kernels for 0%

profile of v1, /device:TPU:0, one launch (start us, length us, event | category | flops | bytes accessed | tf_op | source)
XLA Modules:
  0.0 378.7 jit_solution(17872735415210531985)
XLA Ops:
  7.2 0.0 reduce-scatter.4.cloned.1.call-start
  7.2 0.7 negate_convert_fusion
  7.9 0.7 add_divide_fusion
  8.7 23.5 %all_gather.30 = bf16[512,128]{1,0:T(8,128)(2,1)S(1)} all-gather(bf16[32,128]{1,0:T(8,128)(2,1)S(1)} %negate_convert_fusion), channel_id=1, replica_groups=mesh['groups'=2,'row'=16] {'row'}, dimensions={0}, use_global_device_ids=true | all-gather | bytes 139264 | tf_op jit(solution)/shard_map/all_gather | solution.py:85
  32.1 0.0 copy-start
  32.1 6.4 %fusion.52 = (f32[4096,128]{1,0:T(8,128)S(1)}, f32[4096,128]{1,0:T(8,128)}, f32[4096,128]{1,0:T(8,128)S(1)}) fusion(s32[4096,128]{1,0:T(8,128)} %param.10, s32[4096,128]{1,0:T(8,128)} %param.11, f32[4096,128]{1,0:T(8,128)} %param.8, f32[4096]{0:T(1024)S(1)} %get-tuple-element.64, bf16[512,4096]{1,0:T(8,128)(2,1)} %param.6, ...), kind=kOutput, calls=%fused_computation.132 | convolution fusion | flops 543162368 | bytes 16941056 | tf_op jit(solution)/shard_map/dot_general | solution.py:46
  38.5 0.0 copy-start.6
  38.5 1.3 copy-done.6
  39.8 0.0 copy-done
  39.8 0.0 copy-start.10
  39.8 0.0 copy-start.9
  39.8 1.9 convolution_bitcast_fusion.5
  41.8 0.0 reduce-scatter.4.cloned.1.call-update
  41.8 0.0 reduce-scatter.6.cloned.1.call-start
  41.8 53.1 %reduce-scatter.4.cloned.1.call-done = f32[32,128]{1,0:T(8,128)} async-done(((f32[512,128]{1,0:T(8,128)}), f32[32,128]{1,0:T(8,128)}) %reduce-scatter.4.cloned.1.call-update) | async-done | bytes 16400 | tf_op jit(solution)/shard_map/reduce_scatter | solution.py:74
  94.9 0.0 copy-done.10
  94.9 0.7 subtract_convert_fusion.2
  95.6 19.7 %all_gather.31 = bf16[512,128]{1,0:T(8,128)(2,1)S(1)} all-gather(bf16[32,128]{1,0:T(8,128)(2,1)S(1)} %subtract_convert_fusion.2), channel_id=1, replica_groups=mesh['groups'=2,'row'=16] {'row'}, dimensions={0}, use_global_device_ids=true | all-gather | bytes 139264 | tf_op jit(solution)/shard_map/all_gather | solution.py:85
  115.4 0.0 copy-done.9
  115.4 8.5 %add_reduce_fusion.9 = (f32[128]{0:T(128)S(1)}, f32[128]{0:T(128)S(1)}, f32[128]{0:T(128)S(1)}, f32[4096,128]{1,0:T(8,128)}, f32[4096,128]{1,0:T(8,128)}, /*index=5*/f32[4096,128]{1,0:T(8,128)}) fusion(f32[4096,128]{1,0:T(8,128)} %get-tuple-element.57, f32[4096,128]{1,0:T(8,128)S(1)} %get-tuple-element.58, s32[4096,128]{1,0:T(8,128)} %param.10, ...), kind=kOutput, calls=%fused_computation.40 | convolution fusion | flops 551026304 | bytes 23234048 | tf_op jit(solution)/shard_map/dot_general | solution.py:46
  123.9 17.5 %all-gather.3 = f32[16,3,128]{2,1,0:T(4,128)S(1)} all-gather(f32[1,3,128]{2,1,0:T(4,128)S(1)} %maximum_bitcast_fusion), channel_id=2, replica_groups=mesh['groups'=2,'row'=16] {'row'}, dimensions={0}, use_global_device_ids=true | all-gather | bytes 26112 | tf_op jit(solution)/shard_map/all_gather | solution.py:106
  141.5 6.9 %convolution_bitcast_fusion.4 = f32[512,128]{1,0:T(8,128)} fusion(bf16[512,4096]{1,0:T(8,128)(2,1)} %param.6, f32[4096,128]{1,0:T(8,128)} %get-tuple-element.70, f32[128]{0:T(128)S(1)} %fusion.24, f32[4096,128]{1,0:T(8,128)S(1)} %get-tuple-element.58, f32[128]{0:T(128)S(1)} %get-tuple-element.48, s32[4096,128]{1,0:T(8,128)} %param.10, ...), kind=kOutput, calls=%fused_computation.45 | convolution fusion | flops 545783808 | bytes 14943232 | tf_op jit(solution)/shard_map/dot_general | solution.py:75
  148.4 0.0 reduce-scatter.6.cloned.1.call-update
  148.4 0.0 reduce-scatter.8.cloned.1.call-start
  148.5 54.2 %reduce-scatter.6.cloned.1.call-done = f32[32,128]{1,0:T(8,128)} async-done(((f32[512,128]{1,0:T(8,128)}), f32[32,128]{1,0:T(8,128)}) %reduce-scatter.6.cloned.1.call-update) | async-done | bytes 16400 | tf_op jit(solution)/shard_map/reduce_scatter | solution.py:74
  202.7 0.7 subtract_convert_fusion.1
  203.4 19.8 %all_gather.34 = bf16[512,128]{1,0:T(8,128)(2,1)S(1)} all-gather(bf16[32,128]{1,0:T(8,128)(2,1)S(1)} %subtract_convert_fusion.1), channel_id=1, replica_groups=mesh['groups'=2,'row'=16] {'row'}, dimensions={0}, use_global_device_ids=true | all-gather | bytes 139264 | tf_op jit(solution)/shard_map/all_gather | solution.py:85
  223.2 10.1 %add_reduce_fusion.6 = (f32[128]{0:T(128)S(1)}, f32[128]{0:T(128)S(1)}, f32[128]{0:T(128)S(1)}, f32[4096,128]{1,0:T(8,128)}, f32[4096,128]{1,0:T(8,128)}, /*index=5*/f32[4096,128]{1,0:T(8,128)}) fusion(f32[4096,128]{1,0:T(8,128)} %get-tuple-element.57, f32[4096,128]{1,0:T(8,128)S(1)} %get-tuple-element.58, f32[4096,128]{1,0:T(8,128)} %get-tuple-element.55, ...), kind=kOutput, calls=%fused_computation.33 | convolution fusion | flops 557317760 | bytes 27429376 | tf_op jit(solution)/shard_map/dot_general | solution.py:46
  233.3 17.7 %all-gather.4 = f32[16,3,128]{2,1,0:T(4,128)S(1)} all-gather(f32[1,3,128]{2,1,0:T(4,128)S(1)} %maximum_bitcast_fusion.1), channel_id=3, replica_groups=mesh['groups'=2,'row'=16] {'row'}, dimensions={0}, use_global_device_ids=true | all-gather | bytes 26112 | tf_op jit(solution)/shard_map/all_gather | solution.py:106
  251.1 0.0 copy-start.1
  251.1 7.1 %fusion.33 = (f32[4096,128]{1,0:T(8,128)S(1)}, f32[4096,128]{1,0:T(8,128)}) fusion(f32[128]{0:T(128)S(1)} %get-tuple-element.69, f32[128]{0:T(128)S(1)} %get-tuple-element.68, f32[4096,128]{1,0:T(8,128)S(1)} %get-tuple-element.58, f32[128]{0:T(128)S(1)} %get-tuple-element.36, s32[4096,128]{1,0:T(8,128)} %param.10, s32[4096,128]{1,0:T(8,128)} %param.11, ...), kind=kLoop, calls=%fused_computation.112 | loop fusion | flops 12058624 | bytes 16778752 | tf_op jit(solution)/shard_map/sub | solution.py:52
  258.2 0.0 copy-start.5
  258.2 1.3 copy-done.5
  259.5 0.0 copy-done.1
  259.5 2.0 convolution_bitcast_fusion.3
  261.5 0.0 reduce-scatter.8.cloned.1.call-update
  261.5 54.2 %reduce-scatter.8.cloned.1.call-done = f32[32,128]{1,0:T(8,128)} async-done(((f32[512,128]{1,0:T(8,128)}), f32[32,128]{1,0:T(8,128)}) %reduce-scatter.8.cloned.1.call-update) | async-done | bytes 16400 | tf_op jit(solution)/shard_map/reduce_scatter | solution.py:74
  315.8 0.7 subtract_convert_fusion
  316.5 19.7 %all_gather.37 = bf16[512,128]{1,0:T(8,128)(2,1)S(1)} all-gather(bf16[32,128]{1,0:T(8,128)(2,1)S(1)} %subtract_convert_fusion), channel_id=1, replica_groups=mesh['groups'=2,'row'=16] {'row'}, dimensions={0}, use_global_device_ids=true | all-gather | bytes 139264 | tf_op jit(solution)/shard_map/all_gather | solution.py:85
  336.3 0.0 copy-start.2
  336.3 0.0 copy-start.3
  336.3 0.0 copy-start.4
  336.3 0.0 copy-start.7
  336.3 0.0 copy-start.8
  336.3 9.4 %fusion.22 = (f32[4096,128]{1,0:T(8,128)S(1)}, f32[4096,128]{1,0:T(8,128)S(1)}, f32[4096,128]{1,0:T(8,128)}) fusion(s32[4096,128]{1,0:T(8,128)} %param.10, s32[4096,128]{1,0:T(8,128)} %param.11, f32[128]{0:T(128)S(1)} %get-tuple-element.69, f32[128]{0:T(128)S(1)} %get-tuple-element.68, f32[4096,128]{1,0:T(8,128)S(1)} %get-tuple-element.58, ...), kind=kOutput, calls=%fused_computation.51 | convolution fusion | flops 550502400 | bytes 27428352 | tf_op jit(solution)/shard_map/dot_general | solution.py:46
  345.7 0.0 copy-done.2
  345.7 0.0 copy-done.3
  345.7 0.0 copy-done.4
  345.7 0.0 copy-done.7
  345.7 0.8 copy-done.8
  346.5 1.1 add_reduce_fusion.3
  347.6 17.5 %all-gather.5 = f32[16,4,128]{2,1,0:T(4,128)S(1)} all-gather(f32[1,4,128]{2,1,0:T(4,128)S(1)} %maximum_bitcast_fusion.2), channel_id=4, replica_groups=mesh['groups'=2,'row'=16] {'row'}, dimensions={0}, use_global_device_ids=true | all-gather | bytes 34816 | tf_op jit(solution)/shard_map/all_gather | solution.py:106
  365.3 6.9 %multiply_add_fusion = (f32[4096,128]{1,0:T(8,128)}, f32[4096,128]{1,0:T(8,128)}) fusion(f32[4096,128]{1,0:T(8,128)} %get-tuple-element.57, f32[128]{0:T(128)S(1)} %get-tuple-element.67, f32[128]{0:T(128)S(1)} %get-tuple-element.66, f32[128]{0:T(128)S(1)} %get-tuple-element.65, f32[128]{0:T(128)S(1)} %get-tuple-element.12, ...), kind=kLoop, calls=%fused_computation.22 | loop fusion | flops 15204352 | bytes 18876416 | tf_op jit(solution)/shard_map/add | solution.py:121
  (17 shorter events, 0.3 us)
Async XLA Ops:
  7.2 87.7 %reduce-scatter.4.cloned.1.call-start = ((), (), s32[]{:S(2)}) async-start(), calls=%async_computation.3 | async-start | bytes 278528 | tf_op jit(solution)/shard_map/reduce_scatter | solution.py:74
  32.1 7.7 %copy-start = (bf16[512,4096]{1,0:T(8,128)(2,1)S(1)}, bf16[512,4096]{1,0:T(8,128)(2,1)}, u32[]{:S(2)}) copy-start(bf16[512,4096]{1,0:T(8,128)(2,1)} %param.6) | copy-start | bytes 12582916
  38.5 1.3 copy-start.6
  39.8 55.1 %copy-start.10 = (f32[32,128]{1,0:T(8,128)S(1)}, f32[32,128]{1,0:T(8,128)}, u32[]{:S(2)}) copy-start(f32[32,128]{1,0:T(8,128)} %param.7) | copy-start | bytes 49156
  39.8 75.6 %copy-start.9 = (f32[4096]{0:T(1024)S(1)}, f32[4096]{0:T(1024)}, u32[]{:S(2)}) copy-start(f32[4096]{0:T(1024)} %param.9) | copy-start | bytes 49156
  41.8 160.9 %reduce-scatter.6.cloned.1.call-start = ((), (), s32[]{:S(2)}) async-start(), calls=%async_computation.4 | async-start | bytes 278528 | tf_op jit(solution)/shard_map/reduce_scatter | solution.py:74
  148.4 167.4 %reduce-scatter.8.cloned.1.call-start = ((), (), s32[]{:S(2)}) async-start(), calls=%async_computation.5 | async-start | bytes 278528 | tf_op jit(solution)/shard_map/reduce_scatter | solution.py:74
  251.1 8.5 %copy-start.1 = (bf16[512,4096]{1,0:T(8,128)(2,1)S(1)}, bf16[512,4096]{1,0:T(8,128)(2,1)}, u32[]{:S(2)}) copy-start(bf16[512,4096]{1,0:T(8,128)(2,1)} %param.6) | copy-start | bytes 12582916
  258.2 1.3 copy-start.5
  336.3 9.4 %copy-start.2 = (f32[4096,128]{1,0:T(8,128)S(1)}, f32[4096,128]{1,0:T(8,128)}, u32[]{:S(2)}) copy-start(f32[4096,128]{1,0:T(8,128)} %get-tuple-element.57) | copy-start | bytes 6291460
  336.3 9.4 %copy-start.3 = (f32[4096,128]{1,0:T(8,128)S(1)}, f32[4096,128]{1,0:T(8,128)}, u32[]{:S(2)}) copy-start(f32[4096,128]{1,0:T(8,128)} %get-tuple-element.54) | copy-start | bytes 6291460
  336.3 9.4 %copy-start.4 = (f32[4096,128]{1,0:T(8,128)S(1)}, f32[4096,128]{1,0:T(8,128)}, u32[]{:S(2)}) copy-start(f32[4096,128]{1,0:T(8,128)} %get-tuple-element.55) | copy-start | bytes 6291460
  336.3 9.5 %copy-start.7 = (f32[4096,128]{1,0:T(8,128)S(1)}, f32[4096,128]{1,0:T(8,128)}, u32[]{:S(2)}) copy-start(f32[4096,128]{1,0:T(8,128)} %get-tuple-element.46) | copy-start | bytes 6291460
  336.3 10.3 %copy-start.8 = (f32[4096,128]{1,0:T(8,128)S(1)}, f32[4096,128]{1,0:T(8,128)}, u32[]{:S(2)}) copy-start(f32[4096,128]{1,0:T(8,128)} %get-tuple-element.47) | copy-start | bytes 6291460
Sparse Core Ops, SparseCore 0:
  41.9 52.9 reduce-scatter.3
  148.5 54.1 reduce-scatter.5
  261.7 54.0 reduce-scatter.7

commit v2 on v1

--- a/solution.py
+++ b/solution.py
@@ -42,6 +42,34 @@
     return [item / total for item in solved]
 
 
+def sum_to_owner(part, count):
+    rows = part.shape[0] // count
+    return jnp.sum(
+        lax.all_to_all(
+            part.astype(jnp.bfloat16).reshape(count, rows, part.shape[1]),
+            "row",
+            0,
+            0,
+            tiled=True,
+        ).astype(jnp.float32),
+        axis=0,
+    )
+
+
+def to_everyone(part, count):
+    got = lax.all_to_all(
+        jnp.broadcast_to(part[None], (count,) + part.shape), "row", 0, 0, tiled=True
+    )
+    return got.reshape((count * part.shape[0],) + part.shape[1:])
+
+
+def sum_everywhere(part, count):
+    got = lax.all_to_all(
+        jnp.broadcast_to(part[None], (count,) + part.shape), "row", 0, 0, tiled=True
+    )
+    return jnp.sum(got, axis=0)
+
+
 def apply_map(design_matrix, misfit, z, u, linear, diag, step_size, lower, upper):
     gradient = lax.dot_general(
         design_matrix,
@@ -61,6 +89,7 @@
     upper = upper_code.astype(jnp.float32) / 64.0
     diag = diagonal[:, None]
     step_size = 1.0 / (rho_plus_lip + diag)
+    count_row = lax.axis_size("row")
     z = jnp.zeros(linear.shape, jnp.float32)
     u = z
     mapped = []
@@ -71,18 +100,16 @@
         if iteration == 0:
             misfit = (-targets).astype(jnp.bfloat16)
         else:
-            product = lax.psum_scatter(
+            product = sum_to_owner(
                 jnp.dot(
                     design_matrix,
                     (z - u).astype(jnp.bfloat16),
                     preferred_element_type=jnp.float32,
                 ),
-                "row",
-                scatter_dimension=0,
-                tiled=True,
+                count_row,
             )
             misfit = (product - targets).astype(jnp.bfloat16)
-        misfit = lax.all_gather(misfit, "row", axis=0, tiled=True)
+        misfit = to_everyone(misfit, count_row)
         boxed, scaled = apply_map(
             design_matrix, misfit, z, u, linear, diag, step_size, lower, upper
         )
@@ -103,7 +130,7 @@
             z, u = boxed, scaled
             continue
         partial = jnp.stack([item for _, item in fresh])
-        whole = jnp.sum(lax.all_gather(partial, "row", axis=0), axis=0)
+        whole = sum_everywhere(partial, count_row)
         for k, (pair, _) in enumerate(fresh):
             gram[pair] = whole[k]
         fresh = []

time: 379 us -> 172 us (0.45)
  waiting for transfers between devices: 162 us -> 7.17 us
  blocking collectives: 135 us -> 90.6 us
  between operations: 13.9 us -> 0.89 us
  starting transfers between devices: 0.12 us -> 7.41 us
    reduce_scatter x3 -> x0, waiting for transfers between devices: 162 us -> none  [per_device(): lax.psum_scatter(jnp.dot(design_matrix, (z - u).astype(jnp.bfloat16), pre...]
    all_gather x7 -> x0, blocking collectives: 135 us -> none  [the longest x4 82.7 us: per_device(): misfit = lax.all_gather(misfit, 'row', axis=0, tiled=True)]
    all_to_all x0 -> x9, blocking collectives: none -> 90.6 us  [the longest x3 31.5 us: sum_to_owner(): lax.all_to_all(part.astype(jnp.bfloat16).reshape(count, rows, part.shape[...]
    all_to_all x0 -> x1, starting transfers between devices: none -> 7.41 us  [to_everyone(): lax.all_to_all(jnp.broadcast_to(part[None], (count,) + part.shape), 'row'...]
    all_to_all x0 -> x1, waiting for transfers between devices: none -> 7.17 us  [to_everyone(): lax.all_to_all(jnp.broadcast_to(part[None], (count,) + part.shape), 'row'...]
  transfers between devices with their start and end apart: 3 -> 1, of which waited for: 3 -> 1; matrix products, arithmetic and copies ran while one was open for 0% -> 0% of each run, Pallas kernels for 0% -> 0%
where the time goes in v2:
time: 172 us
  blocking collectives  90.6 us (53%)
  matrix products  44 us (26%)
  other arithmetic  17 us (10%)
  starting transfers between devices  7.41 us (4%)
  waiting for transfers between devices  7.17 us (4%)
  local copies, waits for them, and re-layouts  4.6 us (3%)
    dot_general x4, matrix products, apply_map(): lax.dot_general(design_matrix, misfit, (((0,), (0,)), ((), ())), preferre...  34.4 us
    all_to_all x3, blocking collectives, sum_to_owner(): lax.all_to_all(part.astype(jnp.bfloat16).reshape(count, rows, part.shape[...  31.5 us
    all_to_all x3, blocking collectives, to_everyone(): lax.all_to_all(jnp.broadcast_to(part[None], (count,) + part.shape), 'row'...  31.5 us
    all_to_all x3, blocking collectives, sum_everywhere(): lax.all_to_all(jnp.broadcast_to(part[None], (count,) + part.shape), 'row'...  27.6 us
    dot_general x3, matrix products, per_device(): jnp.dot(design_matrix, (z - u).astype(jnp.bfloat16), preferred_element_ty...  9.61 us
    all_to_all x1, starting transfers between devices, to_everyone(): lax.all_to_all(jnp.broadcast_to(part[None], (count,) + part.shape), 'row'...  7.41 us
    all_to_all x1, waiting for transfers between devices, to_everyone(): lax.all_to_all(jnp.broadcast_to(part[None], (count,) + part.shape), 'row'...  7.17 us
    sub x1, other arithmetic, apply_map(): point = z - u  7.13 us
  transfers between devices with their start and end apart: 1, of which 1 were waited for; matrix products, arithmetic and copies ran while one was open for 0% of the time, Pallas kernels for 0%

profile of v2, /device:TPU:0, one launch (start us, length us, event | category | flops | bytes accessed | tf_op | source)
XLA Modules:
  0.0 171.6 jit_solution(4909968411435438260)
XLA Ops:
  0.6 0.7 negate_convert_fusion
  1.4 0.7 broadcast_in_dim.14
  2.0 7.4 %all-to-all-start = ((bf16[16,32,128]{2,1,0:T(8,128)(2,1)}), bf16[16,32,128]{2,1,0:T(8,128)(2,1)S(1)}, u32[]{:S(2)}, u32[]{:S(2)}) async-start(bf16[16,32,128]{2,1,0:T(8,128)(2,1)} %broadcast_in_dim.14), calls=%async_computation | async-start | bytes 262144 | tf_op jit(solution)/shard_map/all_to_all | solution.py:60
  9.4 0.7 add_divide_fusion
  10.2 7.2 %all-to-all-done = bf16[16,32,128]{2,1,0:T(8,128)(2,1)S(1)} async-done(((bf16[16,32,128]{2,1,0:T(8,128)(2,1)}), bf16[16,32,128]{2,1,0:T(8,128)(2,1)S(1)}, u32[]{:S(2)}, u32[]{:S(2)}) %all-to-all-start) | async-done | bytes 131104 | tf_op jit(solution)/shard_map/all_to_all | solution.py:60
  17.4 0.0 copy-start
  17.4 6.4 %fusion.55 = (f32[4096,128]{1,0:T(8,128)S(1)}, f32[4096,128]{1,0:T(8,128)}, f32[4096,128]{1,0:T(8,128)S(1)}) fusion(s32[4096,128]{1,0:T(8,128)} %param.10, s32[4096,128]{1,0:T(8,128)} %param.11, f32[4096,128]{1,0:T(8,128)} %param.8, f32[4096]{0:T(1024)S(1)} %get-tuple-element.64, bf16[512,4096]{1,0:T(8,128)(2,1)} %param.6, ...), kind=kOutput, calls=%fused_computation.138 | convolution fusion | flops 543162368 | bytes 16941056 | tf_op jit(solution)/shard_map/dot_general | solution.py:74
  23.7 0.0 copy-start.6
  23.7 1.3 copy-done.6
  25.0 0.0 copy-done
  25.0 0.0 copy-start.10
  25.0 0.0 copy-start.9
  25.0 1.5 fusion.18
  26.6 0.1 copy.23
  26.7 10.5 %all_to_all.50 = bf16[16,32,128]{2,1,0:T(8,128)(2,1)S(1)} all-to-all(bf16[16,32,128]{2,1,0:T(8,128)(2,1)S(1)} %bitcast.92), channel_id=1, replica_groups=mesh['groups'=2,'row'=16] {'row'}, dimensions={0} | all-to-all | bytes 262144 | tf_op jit(solution)/shard_map/all_to_all | solution.py:48
  37.2 0.0 copy-done.10
  37.3 10.5 %all_to_all.51 = bf16[16,32,128]{2,1,0:T(8,128)(2,1)S(1)} all-to-all(bf16[16,32,128]{2,1,0:T(8,128)(2,1)S(1)} %broadcast_in_dim.15), channel_id=1, replica_groups=mesh['groups'=2,'row'=16] {'row'}, dimensions={0} | all-to-all | bytes 262144 | tf_op jit(solution)/shard_map/all_to_all | solution.py:60
  47.8 0.0 copy-done.9
  47.8 8.5 %add_reduce_fusion.9 = (f32[128]{0:T(128)S(1)}, f32[128]{0:T(128)S(1)}, f32[128]{0:T(128)S(1)}, f32[4096,128]{1,0:T(8,128)}, f32[4096,128]{1,0:T(8,128)}, /*index=5*/f32[4096,128]{1,0:T(8,128)}) fusion(f32[4096,128]{1,0:T(8,128)} %get-tuple-element.57, f32[4096,128]{1,0:T(8,128)S(1)} %get-tuple-element.58, s32[4096,128]{1,0:T(8,128)} %param.10, ...), kind=kOutput, calls=%fused_computation.40 | convolution fusion | flops 551026304 | bytes 23234048 | tf_op jit(solution)/shard_map/dot_general | solution.py:74
  56.3 9.2 %all_to_all.52 = f32[16,3,128]{2,1,0:T(4,128)S(1)} all-to-all(f32[16,3,128]{2,1,0:T(4,128)S(1)} %broadcast_in_dim.16), channel_id=1, replica_groups=mesh['groups'=2,'row'=16] {'row'}, dimensions={0} | all-to-all | bytes 49152 | tf_op jit(solution)/shard_map/all_to_all | solution.py:67
  65.6 6.5 %fusion.19 = bf16[512,128]{0,1:T(8,128)(2,1)S(1)} fusion(bf16[512,4096]{1,0:T(8,128)(2,1)} %param.6, f32[4096,128]{1,0:T(8,128)} %get-tuple-element.70, f32[128]{0:T(128)S(1)} %fusion.27, f32[4096,128]{1,0:T(8,128)S(1)} %get-tuple-element.58, f32[128]{0:T(128)S(1)} %get-tuple-element.48, s32[4096,128]{1,0:T(8,128)} %param.10, s32[4096,128]{1,0:T(8,128)} %param.11, ...), kind=kOutput, calls=%fused_computation.48 | convolution fusion | flops 545849344 | bytes 14812160 | tf_op jit(solution)/shard_map/dot_general | solution.py:104
  72.2 0.1 copy.26
  72.3 10.5 %all_to_all.53 = bf16[16,32,128]{2,1,0:T(8,128)(2,1)S(1)} all-to-all(bf16[16,32,128]{2,1,0:T(8,128)(2,1)S(1)} %bitcast.93), channel_id=1, replica_groups=mesh['groups'=2,'row'=16] {'row'}, dimensions={0} | all-to-all | bytes 262144 | tf_op jit(solution)/shard_map/all_to_all | solution.py:48
  82.9 10.5 %all_to_all.54 = bf16[16,32,128]{2,1,0:T(8,128)(2,1)S(1)} all-to-all(bf16[16,32,128]{2,1,0:T(8,128)(2,1)S(1)} %broadcast_in_dim.17), channel_id=1, replica_groups=mesh['groups'=2,'row'=16] {'row'}, dimensions={0} | all-to-all | bytes 262144 | tf_op jit(solution)/shard_map/all_to_all | solution.py:60
  93.4 10.1 %add_reduce_fusion.6 = (f32[128]{0:T(128)S(1)}, f32[128]{0:T(128)S(1)}, f32[128]{0:T(128)S(1)}, f32[4096,128]{1,0:T(8,128)}, f32[4096,128]{1,0:T(8,128)}, /*index=5*/f32[4096,128]{1,0:T(8,128)}) fusion(f32[4096,128]{1,0:T(8,128)} %get-tuple-element.57, f32[4096,128]{1,0:T(8,128)S(1)} %get-tuple-element.58, f32[4096,128]{1,0:T(8,128)} %get-tuple-element.55, ...), kind=kOutput, calls=%fused_computation.33 | convolution fusion | flops 557317760 | bytes 27429376 | tf_op jit(solution)/shard_map/dot_general | solution.py:74
  103.5 9.2 %all_to_all.55 = f32[16,3,128]{2,1,0:T(4,128)S(1)} all-to-all(f32[16,3,128]{2,1,0:T(4,128)S(1)} %broadcast_in_dim.18), channel_id=1, replica_groups=mesh['groups'=2,'row'=16] {'row'}, dimensions={0} | all-to-all | bytes 49152 | tf_op jit(solution)/shard_map/all_to_all | solution.py:67
  112.8 0.0 copy-start.1
  112.8 7.1 %fusion.36 = (f32[4096,128]{1,0:T(8,128)S(1)}, f32[4096,128]{1,0:T(8,128)}) fusion(f32[128]{0:T(128)S(1)} %get-tuple-element.69, f32[128]{0:T(128)S(1)} %get-tuple-element.68, f32[4096,128]{1,0:T(8,128)S(1)} %get-tuple-element.58, f32[128]{0:T(128)S(1)} %get-tuple-element.36, s32[4096,128]{1,0:T(8,128)} %param.10, s32[4096,128]{1,0:T(8,128)} %param.11, ...), kind=kLoop, calls=%fused_computation.118 | loop fusion | flops 12058624 | bytes 16778752 | tf_op jit(solution)/shard_map/sub | solution.py:80
  119.9 0.0 copy-start.5
  119.9 1.3 copy-done.5
  121.2 0.0 copy-done.1
  121.3 1.5 fusion.20
  122.8 0.1 copy.29
  122.9 10.5 %all_to_all.56 = bf16[16,32,128]{2,1,0:T(8,128)(2,1)S(1)} all-to-all(bf16[16,32,128]{2,1,0:T(8,128)(2,1)S(1)} %bitcast.94), channel_id=1, replica_groups=mesh['groups'=2,'row'=16] {'row'}, dimensions={0} | all-to-all | bytes 262144 | tf_op jit(solution)/shard_map/all_to_all | solution.py:48
  133.5 10.5 %all_to_all.57 = bf16[16,32,128]{2,1,0:T(8,128)(2,1)S(1)} all-to-all(bf16[16,32,128]{2,1,0:T(8,128)(2,1)S(1)} %broadcast_in_dim.19), channel_id=1, replica_groups=mesh['groups'=2,'row'=16] {'row'}, dimensions={0} | all-to-all | bytes 262144 | tf_op jit(solution)/shard_map/all_to_all | solution.py:60
  144.0 0.0 copy-start.2
  144.0 0.0 copy-start.3
  144.0 0.0 copy-start.4
  144.0 0.0 copy-start.7
  144.0 0.0 copy-start.8
  144.0 9.4 %fusion.25 = (f32[4096,128]{1,0:T(8,128)S(1)}, f32[4096,128]{1,0:T(8,128)S(1)}, f32[4096,128]{1,0:T(8,128)}) fusion(s32[4096,128]{1,0:T(8,128)} %param.10, s32[4096,128]{1,0:T(8,128)} %param.11, f32[128]{0:T(128)S(1)} %get-tuple-element.69, f32[128]{0:T(128)S(1)} %get-tuple-element.68, f32[4096,128]{1,0:T(8,128)S(1)} %get-tuple-element.58, ...), kind=kOutput, calls=%fused_computation.57 | convolution fusion | flops 550502400 | bytes 27428352 | tf_op jit(solution)/shard_map/dot_general | solution.py:74
  153.4 0.0 copy-done.2
  153.4 0.0 copy-done.3
  153.4 0.0 copy-done.4
  153.4 0.0 copy-done.7
  153.4 0.8 copy-done.8
  154.2 1.1 add_reduce_fusion.3
  155.4 9.2 %all_to_all.58 = f32[16,4,128]{2,1,0:T(4,128)S(1)} all-to-all(f32[16,4,128]{2,1,0:T(4,128)S(1)} %broadcast_in_dim.20), channel_id=1, replica_groups=mesh['groups'=2,'row'=16] {'row'}, dimensions={0} | all-to-all | bytes 65536 | tf_op jit(solution)/shard_map/all_to_all | solution.py:67
  164.7 6.9 %multiply_add_fusion = (f32[4096,128]{1,0:T(8,128)}, f32[4096,128]{1,0:T(8,128)}) fusion(f32[4096,128]{1,0:T(8,128)} %get-tuple-element.57, f32[128]{0:T(128)S(1)} %get-tuple-element.67, f32[128]{0:T(128)S(1)} %get-tuple-element.66, f32[128]{0:T(128)S(1)} %get-tuple-element.65, f32[128]{0:T(128)S(1)} %get-tuple-element.12, ...), kind=kLoop, calls=%fused_computation.22 | loop fusion | flops 15204352 | bytes 18876416 | tf_op jit(solution)/shard_map/add | solution.py:148
  (29 shorter events, 0.5 us)
Async XLA Ops:
  2.0 15.3 %all-to-all-start = ((bf16[16,32,128]{2,1,0:T(8,128)(2,1)}), bf16[16,32,128]{2,1,0:T(8,128)(2,1)S(1)}, u32[]{:S(2)}, u32[]{:S(2)}) async-start(bf16[16,32,128]{2,1,0:T(8,128)(2,1)} %broadcast_in_dim.14), calls=%async_computation | async-start | bytes 262144 | tf_op jit(solution)/shard_map/all_to_all | solution.py:60
  17.4 7.7 %copy-start = (bf16[512,4096]{1,0:T(8,128)(2,1)S(1)}, bf16[512,4096]{1,0:T(8,128)(2,1)}, u32[]{:S(2)}) copy-start(bf16[512,4096]{1,0:T(8,128)(2,1)} %param.6) | copy-start | bytes 12582916
  23.7 1.3 copy-start.6
  25.0 12.2 %copy-start.10 = (f32[32,128]{1,0:T(8,128)S(1)}, f32[32,128]{1,0:T(8,128)}, u32[]{:S(2)}) copy-start(f32[32,128]{1,0:T(8,128)} %param.7) | copy-start | bytes 49156
  25.0 22.7 %copy-start.9 = (f32[4096]{0:T(1024)S(1)}, f32[4096]{0:T(1024)}, u32[]{:S(2)}) copy-start(f32[4096]{0:T(1024)} %param.9) | copy-start | bytes 49156
  112.8 8.5 %copy-start.1 = (bf16[512,4096]{1,0:T(8,128)(2,1)S(1)}, bf16[512,4096]{1,0:T(8,128)(2,1)}, u32[]{:S(2)}) copy-start(bf16[512,4096]{1,0:T(8,128)(2,1)} %param.6) | copy-start | bytes 12582916
  119.9 1.3 copy-start.5
  144.0 9.4 %copy-start.2 = (f32[4096,128]{1,0:T(8,128)S(1)}, f32[4096,128]{1,0:T(8,128)}, u32[]{:S(2)}) copy-start(f32[4096,128]{1,0:T(8,128)} %get-tuple-element.57) | copy-start | bytes 6291460
  144.0 9.4 %copy-start.3 = (f32[4096,128]{1,0:T(8,128)S(1)}, f32[4096,128]{1,0:T(8,128)}, u32[]{:S(2)}) copy-start(f32[4096,128]{1,0:T(8,128)} %get-tuple-element.54) | copy-start | bytes 6291460
  144.0 9.4 %copy-start.4 = (f32[4096,128]{1,0:T(8,128)S(1)}, f32[4096,128]{1,0:T(8,128)}, u32[]{:S(2)}) copy-start(f32[4096,128]{1,0:T(8,128)} %get-tuple-element.55) | copy-start | bytes 6291460
  144.0 9.4 %copy-start.7 = (f32[4096,128]{1,0:T(8,128)S(1)}, f32[4096,128]{1,0:T(8,128)}, u32[]{:S(2)}) copy-start(f32[4096,128]{1,0:T(8,128)} %get-tuple-element.46) | copy-start | bytes 6291460
  144.0 10.3 %copy-start.8 = (f32[4096,128]{1,0:T(8,128)S(1)}, f32[4096,128]{1,0:T(8,128)}, u32[]{:S(2)}) copy-start(f32[4096,128]{1,0:T(8,128)} %get-tuple-element.47) | copy-start | bytes 6291460
